TPU v7x, 32 devices: a whole 2x2x4 slice. The times are simulated.
32 devices in a mesh: row: 4 (over x, core), col: 8 (over z, y).
Axes of the slice: x: 2, y: 2, z: 4, core: 2. Of those that a mesh axis runs over, the one named last changes fastest.
Arguments:
- weight: bfloat16 [8192, 16384], P('row', 'col'), may hold values from -6 to 6
- gradient: bfloat16 [8192, 16384], P('row', 'col'), may hold values from -6 to 6
- old_basis: bfloat16 [8192, 1024], P('row'), may hold values from -0.0625 to 0.0625
- new_basis: bfloat16 [8192, 1024], P('row'), may hold values from -0.0625 to 0.0625
- first_moment: float32 [1024, 16384], P(None, ('col', 'row')), may hold values from -6 to 6
- second_moment: float32 [1024, 16384], P(None, ('col', 'row')), may hold values from 0.05 to 2
Outputs:
- new_weight: bfloat16 [8192, 16384], P('row', 'col')
- update: bfloat16 [8192, 16384], P('row', 'col')
- first_new: float32 [1024, 16384], P(None, ('col', 'row'))
- second_new: float32 [1024, 16384], P(None, ('col', 'row'))
All inputs are finite; a program needn't handle non-finite values.
Results may differ from a plain program's by a relative error of at most 0.0047.
Values may be sent and summed in bfloat16 or wider, within the bound.
A program may use at most 128 MiB of HBM per device.

v0:
```python
import jax
import jax.numpy as jnp
from jax import lax
from jax.sharding import PartitionSpec as P

beta_first = 0.9
beta_second = 0.95
epsilon = 1e-08
step_rate = 0.0025


def low(values):
    return values.astype(jnp.bfloat16)


def wide(values):
    return values.astype(jnp.float32)


def product(left, right):
    return jnp.einsum("mr,mn->rn", left, right, preferred_element_type=jnp.float32)


def transposed_transition(columns, old_basis, new_basis):
    part = old_basis.shape[1] // columns
    mine = lax.dynamic_slice_in_dim(old_basis, lax.axis_index("col") * part, part, axis=1)
    summed = lax.psum(product(mine, new_basis), "row")
    return lax.all_gather(low(summed), "col", axis=0, tiled=True)


def swaps(rows):
    core = [(r, r ^ 1) for r in range(rows)]
    chip = [(r, r ^ 2) for r in range(rows)]
    return (core, chip)


def shards(rows, columns, weight, gradient, old_basis, new_basis, first_moment, second_moment):
    flipped = transposed_transition(columns, old_basis, new_basis)
    squares = low(jnp.square(wide(flipped)))
    moved_first = product(flipped, low(first_moment))
    moved_second = product(squares, low(second_moment))
    width = first_moment.shape[1]
    row = lax.axis_index("row")
    here, core_mate, chip_mate, diagonal = (row ^ k for k in range(4)) if rows == 4 else (row,) * 4
    if rows == 4:
        core, chip = swaps(rows)

        def partial(block):
            piece = lax.dynamic_slice_in_dim(gradient, block * width, width, axis=1)
            return product(new_basis, piece)

        to_core_far = lax.ppermute(low(partial(diagonal)), "row", core)
        far = low(partial(chip_mate) + wide(to_core_far))
        from_chip = lax.ppermute(far, "row", chip)
        from_core = lax.ppermute(low(partial(core_mate)), "row", core)
        projected = partial(here) + wide(from_core) + wide(from_chip)
    else:
        sums = low(product(new_basis, gradient))
        projected = wide(lax.psum_scatter(sums, "row", scatter_dimension=1, tiled=True))
    first_new = beta_first * moved_first + (1.0 - beta_first) * projected
    second_new = beta_second * moved_second + (1.0 - beta_second) * projected * projected
    direction = low(first_new / (jnp.sqrt(second_new) + epsilon))
    if rows == 4:
        across = lax.ppermute(direction, "row", chip)
        beside = lax.ppermute(direction, "row", core)
        beyond = lax.ppermute(across, "row", core)
        directions = jnp.zeros((direction.shape[0], width * rows), direction.dtype)
        for block, values in (
            (here, direction),
            (core_mate, beside),
            (chip_mate, across),
            (diagonal, beyond),
        ):
            directions = lax.dynamic_update_slice_in_dim(directions, values, block * width, axis=1)
    else:
        directions = lax.all_gather(direction, "row", axis=1, tiled=True)
    back = jnp.dot(new_basis, directions, preferred_element_type=jnp.float32)
    new_weight = low(wide(weight) - step_rate * back)
    return (new_weight, low(back), first_new, second_new)


def solution(mesh):
    placed = (
        P("row", "col"),
        P("row", "col"),
        P("row", None),
        P("row", None),
        P(None, ("col", "row")),
        P(None, ("col", "row")),
    )
    return jax.shard_map(
        lambda *blocks: shards(mesh.shape["row"], mesh.shape["col"], *blocks),
        mesh=mesh,
        in_specs=placed,
        out_specs=(
            P("row", "col"),
            P("row", "col"),
            P(None, ("col", "row")),
            P(None, ("col", "row")),
        ),
        check_vma=False,
    )
```

profile of v0, /device:TPU:1, one launch (start us, length us, event | category | flops | bytes accessed | tf_op | source)
XLA Modules:
  0.0 180.5 jit_solution(16227457285369847139)
XLA Ops:
  7.2 0.0 all-gather.2.cloned.1.call-start
  7.2 3.1 %fusion.29 = f32[128,1024]{1,0:T(8,128)S(1)} fusion(bf16[2048,1024]{1,0:T(8,128)(2,1)} %param.9, bf16[2048,1024]{1,0:T(8,128)(2,1)} %param.8, s32[]{:T(128)S(6)} %select_n.19), kind=kOutput, calls=%fused_computation.27 | convolution fusion | flops 536870912 | bytes 5242884 | tf_op jit(solution)/shard_map/mr,mn->rn/dot_general | solution.py:21
  10.3 17.3 %all-reduce.1 = bf16[128,1024]{1,0:T(8,128)(2,1)} all-reduce(f32[128,1024]{1,0:T(8,128)S(1)} %fusion.29), channel_id=1, replica_groups=mesh['row'=4,'col'=8] {'row'}, use_global_device_ids=true, to_apply=%region_0.0 | all-reduce | flops 131072 | bytes 786432 | tf_op jit(solution)/shard_map/psum | solution.py:27
  27.6 0.0 all-gather.2.cloned.1.call-update
  27.6 5.2 %fusion.21 = bf16[1024,512]{1,0:T(8,128)(2,1)S(1)} fusion(bf16[2048,1024]{1,0:T(8,128)(2,1)} %param.9, bf16[2048,2048]{1,0:T(8,128)(2,1)} %param.7, s32[]{:T(128)S(6)} %select_n.23), kind=kOutput, calls=%fused_computation.23 | convolution fusion | flops 2148007936 | bytes 7340036 | tf_op jit(solution)/shard_map/mr,mn->rn/dot_general | solution.py:21
  32.9 1.9 %collective-permute-start.1 = (bf16[1024,512]{1,0:T(8,128)(2,1)S(1)}, bf16[1024,512]{1,0:T(8,128)(2,1)S(1)}, u32[]{:S(2)}, u32[]{:S(2)}) collective-permute-start(bf16[1024,512]{1,0:T(8,128)(2,1)S(1)} %fusion.21), channel_id=1, source_target_pairs={{0,8},{8,0},{16,24},{24,16},{1,9},{9,1},{17,25},{25,17},{2,10},{10... | collective-permute-start | bytes 3145736 | tf_op jit(solution)/shard_map/ppermute | solution.py:52
  34.7 6.3 %fusion.24 = bf16[1024,512]{1,0:T(8,128)(2,1)} fusion(bf16[2048,1024]{1,0:T(8,128)(2,1)} %param.9, bf16[2048,2048]{1,0:T(8,128)(2,1)} %param.7, s32[]{:T(128)S(6)} %select_n.21), kind=kOutput, calls=%fused_computation.24 | convolution fusion | flops 2148007936 | bytes 7340036 | tf_op jit(solution)/shard_map/mr,mn->rn/dot_general | solution.py:21
  41.0 0.0 collective-permute-start
  41.0 0.0 collective-permute-done.1
  41.0 6.2 %fusion.3 = bf16[1024,512]{1,0:T(8,128)(2,1)} fusion(bf16[1024,512]{1,0:T(8,128)(2,1)S(1)} %collective-permute-done.1, bf16[2048,1024]{1,0:T(8,128)(2,1)} %param.9, bf16[2048,2048]{1,0:T(8,128)(2,1)} %param.7, s32[]{:T(128)S(6)} %select_n.22), kind=kOutput, calls=%fused_computation.8 | convolution fusion | flops 2149056512 | bytes 8388612 | tf_op jit(solution)/shard_map/mr,mn->rn/dot_general | solution.py:21
  47.2 0.6 collective-permute-start.2
  47.8 0.0 copy-start.1
  47.8 6.7 %fusion.11 = f32[512,1024]{0,1:T(8,128)} fusion(bf16[2048,1024]{1,0:T(8,128)(2,1)} %param.9, bf16[2048,2048]{1,0:T(8,128)(2,1)} %param.7, s32[]{:T(128)S(6)} %select_n.20), kind=kOutput, calls=%fused_computation.19 | convolution fusion | flops 2147483648 | bytes 8388612 | tf_op jit(solution)/shard_map/mr,mn->rn/dot_general | solution.py:21
  54.5 0.0 collective-permute-done
  54.5 17.3 %collective-permute-done.2 = bf16[1024,512]{1,0:T(8,128)(2,1)} collective-permute-done((bf16[1024,512]{1,0:T(8,128)(2,1)}, bf16[1024,512]{1,0:T(8,128)(2,1)}, u32[]{:S(2)}, u32[]{:S(2)}) %collective-permute-start.2) | collective-permute-done | bytes 1048608 | tf_op jit(solution)/shard_map/ppermute | solution.py:54
  71.8 4.9 %all-gather.2.cloned.1.call-done = bf16[1024,1024]{1,0:T(8,128)(2,1)} async-done(((bf16[128,1024]{1,0:T(8,128)(2,1)}), bf16[1024,1024]{1,0:T(8,128)(2,1)}) %all-gather.2.cloned.1.call-update) | async-done | bytes 2097168 | tf_op jit(solution)/shard_map/all_gather | solution.py:28
  76.7 0.0 copy-done.1
  76.7 0.0 copy-start.5
  76.7 4.2 %fusion.1 = f32[1024,512]{1,0:T(8,128)S(1)} fusion(bf16[1024,1024]{1,0:T(8,128)(2,1)} %all-gather.2.cloned.1.call-done, f32[1024,512]{1,0:T(8,128)S(1)} %copy-done.1, bf16[1024,512]{1,0:T(8,128)(2,1)} %collective-permute-done.2, bf16[1024,512]{1,0:T(8,128)(2,1)S(1)} %collective-permute-done, f32[512,1024]{0,1:T(8,128)} %fusion.11), kind=kOutput, calls=%fused_computation.5 | convolution fusion | flops 1081606144 | bytes 10485760 | tf_op jit(solution)/shard_map/mr,mn->rn/dot_general | solution.py:21
  80.9 0.0 copy-start.4
  80.9 0.0 copy-start.2
  80.9 0.0 copy-start.3
  81.0 2.7 %broadcast_in_dim.3 = bf16[1024,2048]{1,0:T(8,128)(2,1)} broadcast(bf16[]{:T(256)} %constant.17.clone.1), dimensions={} | broadcast | bytes 4194306 | tf_op jit(solution)/shard_map/broadcast_in_dim | solution.py:67
  83.6 0.0 copy-done.5
  83.6 0.5 copy-done.2
  84.1 1.3 copy-done.3
  85.4 5.5 %constant_dynamic-update-slice_fusion.3 = (bf16[1024,2048]{1,0:T(8,128)(2,1)}, bf16[1024,512]{1,0:T(8,128)(2,1)}, f32[1024,512]{1,0:T(8,128)}) fusion(bf16[1024,2048]{1,0:T(8,128)(2,1)} %broadcast_in_dim.3, s32[]{:T(128)S(6)} %select_n.20, f32[1024,512]{1,0:T(8,128)S(1)} %fusion.1, bf16[1024,512]{1,0:T(8,128)(2,1)} %collective-permute-done.2, ...), kind=kOutput, calls=%fused_computation.32 | convolution fusion | flops 1079508992 | bytes 14680068 | tf_op jit(solution)/shard_map/mr,mn->rn/dot_general | solution.py:21
  91.0 0.0 copy-done.4
  91.0 1.2 collective-permute-start.4
  92.2 2.9 %collective-permute-start.3 = (bf16[1024,512]{1,0:T(8,128)(2,1)}, bf16[1024,512]{1,0:T(8,128)(2,1)S(1)}, u32[]{:S(2)}, u32[]{:S(2)}) collective-permute-start(bf16[1024,512]{1,0:T(8,128)(2,1)} %get-tuple-element.9), channel_id=1, source_target_pairs={{0,8},{8,0},{16,24},{24,16},{1,9},{9,1},{17,25},{25,17},{2,10},{10... | collective-permute-start | bytes 3145736 | tf_op jit(solution)/shard_map/ppermute | solution.py:65
  95.0 18.3 %collective-permute-done.4 = bf16[1024,512]{1,0:T(8,128)(2,1)S(1)} collective-permute-done((bf16[1024,512]{1,0:T(8,128)(2,1)}, bf16[1024,512]{1,0:T(8,128)(2,1)S(1)}, u32[]{:S(2)}, u32[]{:S(2)}) %collective-permute-start.4) | collective-permute-done | bytes 1048608 | tf_op jit(solution)/shard_map/ppermute | solution.py:64
  113.3 3.4 %collective-permute-start.5 = (bf16[1024,512]{1,0:T(8,128)(2,1)S(1)}, bf16[1024,512]{1,0:T(8,128)(2,1)S(1)}, u32[]{:S(2)}, u32[]{:S(2)}) collective-permute-start(bf16[1024,512]{1,0:T(8,128)(2,1)S(1)} %collective-permute-done.4), channel_id=1, source_target_pairs={{0,8},{8,0},{16,24},{24,16},{1,9},{9,1},{17,25},{25,17},{2,10},{10... | collective-permute-start | bytes 3145736 | tf_op jit(solution)/shard_map/ppermute | solution.py:66
  116.8 12.2 %copy.10 = bf16[2048,2048]{0,1:T(8,128)(2,1)} copy(bf16[2048,2048]{1,0:T(8,128)(2,1)} %param.6) | data formatting | bytes 16777216 | tf_op args[0]
  129.0 0.0 copy-start
  129.0 0.0 collective-permute-done.3
  129.0 1.0 constant_dynamic-update-slice_fusion.2
  130.0 1.0 constant_dynamic-update-slice_fusion.1
  131.1 0.0 collective-permute-done.5
  131.1 1.0 constant_dynamic-update-slice_fusion
  132.1 0.0 copy-done
  132.1 17.1 %fusion = (bf16[2048,2048]{0,1:T(8,128)(2,1)}, bf16[2048,2048]{1,0:T(8,128)(2,1)}) fusion(bf16[2048,2048]{0,1:T(8,128)(2,1)} %copy.10, bf16[1024,2048]{1,0:T(8,128)(2,1)} %constant_dynamic-update-slice_fusion, bf16[2048,1024]{1,0:T(8,128)(2,1)S(1)} %copy-done), kind=kOutput, calls=%fused_computation.1 | convolution fusion | flops 8610906112 | bytes 33554432 | tf_op jit(solution)/shard_map/dot_general | solution.py:77
  149.2 12.2 %copy.15 = bf16[2048,2048]{1,0:T(8,128)(2,1)} copy(bf16[2048,2048]{0,1:T(8,128)(2,1)} %get-tuple-element.11) | data formatting | bytes 16777216
  161.5 12.2 %copy.16 = bf16[2048,2048]{1,0:T(8,128)(2,1)} copy(bf16[2048,2048]{0,1:T(8,128)(2,1)} %bitcast.31) | data formatting | bytes 16777216
Async XLA Ops:
  7.2 69.5 %all-gather.2.cloned.1.call-start = ((), (), s32[]{:S(2)}) async-start(), calls=%async_computation | async-start | bytes 2359296 | tf_op jit(solution)/shard_map/all_gather | solution.py:28
  32.9 8.1 %collective-permute-start.1 = (bf16[1024,512]{1,0:T(8,128)(2,1)S(1)}, bf16[1024,512]{1,0:T(8,128)(2,1)S(1)}, u32[]{:S(2)}, u32[]{:S(2)}) collective-permute-start(bf16[1024,512]{1,0:T(8,128)(2,1)S(1)} %fusion.21), channel_id=1, source_target_pairs={{0,8},{8,0},{16,24},{24,16},{1,9},{9,1},{17,25},{25,17},{2,10},{10... | collective-permute-start | bytes 3145736 | tf_op jit(solution)/shard_map/ppermute | solution.py:52
  41.0 13.5 %collective-permute-start = (bf16[1024,512]{1,0:T(8,128)(2,1)}, bf16[1024,512]{1,0:T(8,128)(2,1)S(1)}, u32[]{:S(2)}, u32[]{:S(2)}) collective-permute-start(bf16[1024,512]{1,0:T(8,128)(2,1)} %fusion.24), channel_id=1, source_target_pairs={{0,8},{8,0},{16,24},{24,16},{1,9},{9,1},{17,25},{25,17},{2,10},{10... | collective-permute-start | bytes 3145736 | tf_op jit(solution)/shard_map/ppermute | solution.py:55
  47.2 24.5 %collective-permute-start.2 = (bf16[1024,512]{1,0:T(8,128)(2,1)}, bf16[1024,512]{1,0:T(8,128)(2,1)}, u32[]{:S(2)}, u32[]{:S(2)}) collective-permute-start(bf16[1024,512]{1,0:T(8,128)(2,1)} %fusion.3), channel_id=1, source_target_pairs={{0,16},{8,24},{16,0},{24,8},{1,17},{9,25},{17,1},{25,9},{2,18},{10... | collective-permute-start | bytes 3145736 | tf_op jit(solution)/shard_map/ppermute | solution.py:54
  47.8 28.9 %copy-start.1 = (f32[1024,512]{1,0:T(8,128)S(1)}, f32[1024,512]{1,0:T(8,128)}, u32[]{:S(2)}) copy-start(f32[1024,512]{1,0:T(8,128)} %param.11) | copy-start | bytes 6291460
  76.7 6.9 %copy-start.5 = (f32[512,1024]{0,1:T(8,128)S(1)}, f32[512,1024]{0,1:T(8,128)}, u32[]{:S(2)}) copy-start(f32[512,1024]{0,1:T(8,128)} %fusion.11) | copy-start | bytes 6291460
  80.9 10.0 %copy-start.4 = (f32[1024,512]{1,0:T(8,128)}, f32[1024,512]{1,0:T(8,128)S(1)}, u32[]{:S(2)}) copy-start(f32[1024,512]{1,0:T(8,128)S(1)} %fusion.1) | copy-start | bytes 6291460
  80.9 3.2 %copy-start.2 = (f32[1024,512]{1,0:T(8,128)S(1)}, f32[1024,512]{1,0:T(8,128)}, u32[]{:S(2)}) copy-start(f32[1024,512]{1,0:T(8,128)} %param.10) | copy-start | bytes 6291460
  80.9 4.5 %copy-start.3 = (bf16[1024,1024]{1,0:T(8,128)(2,1)S(1)}, bf16[1024,1024]{1,0:T(8,128)(2,1)}, u32[]{:S(2)}) copy-start(bf16[1024,1024]{1,0:T(8,128)(2,1)} %all-gather.2.cloned.1.call-done) | copy-start | bytes 6291460
  91.0 22.3 %collective-permute-start.4 = (bf16[1024,512]{1,0:T(8,128)(2,1)}, bf16[1024,512]{1,0:T(8,128)(2,1)S(1)}, u32[]{:S(2)}, u32[]{:S(2)}) collective-permute-start(bf16[1024,512]{1,0:T(8,128)(2,1)} %get-tuple-element.9), channel_id=1, source_target_pairs={{0,16},{8,24},{16,0},{24,8},{1,17},{9,25},{17,1},{25,9},{2,18},{10... | collective-permute-start | bytes 3145736 | tf_op jit(solution)/shard_map/ppermute | solution.py:64
  92.2 36.8 %collective-permute-start.3 = (bf16[1024,512]{1,0:T(8,128)(2,1)}, bf16[1024,512]{1,0:T(8,128)(2,1)S(1)}, u32[]{:S(2)}, u32[]{:S(2)}) collective-permute-start(bf16[1024,512]{1,0:T(8,128)(2,1)} %get-tuple-element.9), channel_id=1, source_target_pairs={{0,8},{8,0},{16,24},{24,16},{1,9},{9,1},{17,25},{25,17},{2,10},{10... | collective-permute-start | bytes 3145736 | tf_op jit(solution)/shard_map/ppermute | solution.py:65
  113.3 17.8 %collective-permute-start.5 = (bf16[1024,512]{1,0:T(8,128)(2,1)S(1)}, bf16[1024,512]{1,0:T(8,128)(2,1)S(1)}, u32[]{:S(2)}, u32[]{:S(2)}) collective-permute-start(bf16[1024,512]{1,0:T(8,128)(2,1)S(1)} %collective-permute-done.4), channel_id=1, source_target_pairs={{0,8},{8,0},{16,24},{24,16},{1,9},{9,1},{17,25},{25,17},{2,10},{10... | collective-permute-start | bytes 3145736 | tf_op jit(solution)/shard_map/ppermute | solution.py:66
  129.0 3.1 %copy-start = (bf16[2048,1024]{1,0:T(8,128)(2,1)S(1)}, bf16[2048,1024]{1,0:T(8,128)(2,1)}, u32[]{:S(2)}) copy-start(bf16[2048,1024]{1,0:T(8,128)(2,1)} %param.9) | copy-start | bytes 12582916
Sparse Core Ops, SparseCore 0:
  27.7 48.8 all-gather.1
where the time goes:
time: 182 us; the launch traced here: 181 us
  matrix products  54.4 us (30%)
  local copies, waits for them, and re-layouts  44.3 us (24%)
  waiting for transfers between devices  40.5 us (22%)
  blocking collectives  17.3 us (10%)
  between operations  14.1 us (8%)
  starting transfers between devices  10 us (5%)
    unnamed x15, local copies, waits for them, and re-layouts  38.5 us
    dot_general x7, matrix products, product(): jnp.einsum('mr,mn->rn', left, right, preferred_element_type=jnp.float32)  37.2 us
    ppermute x1, waiting for transfers between devices, shards(): across = lax.ppermute(direction, 'row', chip)  18.3 us
    ppermute x1, waiting for transfers between devices, shards(): from_chip = lax.ppermute(far, 'row', chip)  17.3 us
    psum x1, blocking collectives, transposed_transition(): summed = lax.psum(product(mine, new_basis), 'row')  17.3 us
    dot_general x1, matrix products, shards(): back = jnp.dot(new_basis, directions, preferred_element_type=jnp.float32)  17.1 us
    all_gather x1, waiting for transfers between devices, transposed_transition(): return lax.all_gather(low(summed), 'col', axis=0, tiled=True)  4.92 us
  transfers between devices with their start and end apart: 7, of which 3 were waited for; matrix products, arithmetic and copies ran while one was open for 21% of the time, Pallas kernels for 0%

commit v1 on v0

--- a/solution.py
+++ b/solution.py
@@ -24,7 +24,7 @@
 def transposed_transition(columns, old_basis, new_basis):
     part = old_basis.shape[1] // columns
     mine = lax.dynamic_slice_in_dim(old_basis, lax.axis_index("col") * part, part, axis=1)
-    summed = lax.psum(product(mine, new_basis), "row")
+    summed = jnp.sum(lax.all_gather(product(mine, new_basis), "row"), axis=0)
     return lax.all_gather(low(summed), "col", axis=0, tiled=True)
 
 

time: 182 us -> 191 us (1.049)
  waiting for transfers between devices: 40.5 us -> 65.3 us
  blocking collectives: 17.3 us -> 0 us
  other arithmetic: 0 us -> 2.53 us
    all_gather x0 -> x1, waiting for transfers between devices: none -> 25.1 us  [transposed_transition(): summed = jnp.sum(lax.all_gather(product(mine, new_basis), 'row'), axis=0)]
    psum x1 -> x0, blocking collectives: 17.3 us -> none  [transposed_transition(): summed = lax.psum(product(mine, new_basis), 'row')]
    reduce_sum x0 -> x1, other arithmetic: none -> 2.53 us  [transposed_transition(): summed = jnp.sum(lax.all_gather(product(mine, new_basis), 'row'), axis=0)]
  transfers between devices with their start and end apart: 7 -> 8, of which waited for: 3 -> 4; matrix products, arithmetic and copies ran while one was open for 21% -> 20% of each run, Pallas kernels for 0% -> 0%
where the time goes in v1:
time: 191 us; the launch traced here: 190 us
  waiting for transfers between devices  65.3 us (34%)
  matrix products  55.3 us (29%)
  local copies, waits for them, and re-layouts  44.3 us (23%)
  between operations  14.1 us (7%)
  starting transfers between devices  8.18 us (4%)
  other arithmetic  2.53 us (1%)
    unnamed x15, local copies, waits for them, and re-layouts  38.5 us
    dot_general x7, matrix products, product(): jnp.einsum('mr,mn->rn', left, right, preferred_element_type=jnp.float32)  38.1 us
    all_gather x1, waiting for transfers between devices, transposed_transition(): summed = jnp.sum(lax.all_gather(product(mine, new_basis), 'row'), axis=0)  25.1 us
    ppermute x1, waiting for transfers between devices, shards(): across = lax.ppermute(direction, 'row', chip)  18.3 us
    ppermute x1, waiting for transfers between devices, shards(): from_chip = lax.ppermute(far, 'row', chip)  18.1 us
    dot_general x1, matrix products, shards(): back = jnp.dot(new_basis, directions, preferred_element_type=jnp.float32)  17.1 us
  transfers between devices with their start and end apart: 8, of which 4 were waited for; matrix products, arithmetic and copies ran while one was open for 20% of the time, Pallas kernels for 0%

profile of v1, /device:TPU:1, one launch (start us, length us, event | category | flops | bytes accessed | tf_op | source)
XLA Modules:
  0.0 189.7 jit_solution(9705743622113435033)
XLA Ops:
  7.2 0.0 all-gather.6.cloned.1.call-start
  7.2 3.9 %fusion.29 = f32[128,1024]{1,0:T(8,128)} fusion(bf16[2048,1024]{1,0:T(8,128)(2,1)} %param.9, bf16[2048,1024]{1,0:T(8,128)(2,1)} %param.8, s32[]{:T(128)S(6)} %select_n.19), kind=kOutput, calls=%fused_computation.27 | convolution fusion | flops 536870912 | bytes 5242884 | tf_op jit(solution)/shard_map/mr,mn->rn/dot_general | solution.py:21
  11.1 0.0 all-gather.6.cloned.1.call-update
  11.2 0.0 all-gather.4.cloned.1.call-start
  11.2 25.1 %all-gather.6.cloned.1.call-done = f32[512,1024]{1,0:T(8,128)} async-done(((f32[128,1024]{1,0:T(8,128)}), f32[512,1024]{1,0:T(8,128)}) %all-gather.6.cloned.1.call-update) | async-done | bytes 2097168 | tf_op jit(solution)/shard_map/all_gather | solution.py:27
  36.3 2.5 %reduce_sum.9 = bf16[128,1024]{1,0:T(8,128)(2,1)} reduce(f32[4,128,1024]{2,1,0:T(8,128)} %bitcast.33, f32[]{:T(128)} %constant.7.clone.1), dimensions={0}, to_apply=%region_0.0 | reduce | flops 393216 | bytes 2359300 | tf_op jit(solution)/shard_map/reduce_sum | solution.py:27
  38.9 0.0 all-gather.4.cloned.1.call-update
  38.9 5.2 %fusion.21 = bf16[1024,512]{1,0:T(8,128)(2,1)S(1)} fusion(bf16[2048,1024]{1,0:T(8,128)(2,1)} %param.9, bf16[2048,2048]{1,0:T(8,128)(2,1)} %param.7, s32[]{:T(128)S(6)} %select_n.23), kind=kOutput, calls=%fused_computation.23 | convolution fusion | flops 2148007936 | bytes 7340036 | tf_op jit(solution)/shard_map/mr,mn->rn/dot_general | solution.py:21
  44.1 0.3 collective-permute-start.1
  44.5 6.3 %fusion.24 = bf16[1024,512]{1,0:T(8,128)(2,1)} fusion(bf16[2048,1024]{1,0:T(8,128)(2,1)} %param.9, bf16[2048,2048]{1,0:T(8,128)(2,1)} %param.7, s32[]{:T(128)S(6)} %select_n.21), kind=kOutput, calls=%fused_computation.24 | convolution fusion | flops 2148007936 | bytes 7340036 | tf_op jit(solution)/shard_map/mr,mn->rn/dot_general | solution.py:21
  50.8 0.2 collective-permute-start
  51.0 0.0 collective-permute-done.1
  51.0 6.2 %fusion.3 = bf16[1024,512]{1,0:T(8,128)(2,1)} fusion(bf16[1024,512]{1,0:T(8,128)(2,1)S(1)} %collective-permute-done.1, bf16[2048,1024]{1,0:T(8,128)(2,1)} %param.9, bf16[2048,2048]{1,0:T(8,128)(2,1)} %param.7, s32[]{:T(128)S(6)} %select_n.22), kind=kOutput, calls=%fused_computation.8 | convolution fusion | flops 2149056512 | bytes 8388612 | tf_op jit(solution)/shard_map/mr,mn->rn/dot_general | solution.py:21
  57.3 0.0 collective-permute-start.2
  57.3 0.0 copy-start.1
  57.3 6.7 %fusion.11 = f32[512,1024]{0,1:T(8,128)} fusion(bf16[2048,1024]{1,0:T(8,128)(2,1)} %param.9, bf16[2048,2048]{1,0:T(8,128)(2,1)} %param.7, s32[]{:T(128)S(6)} %select_n.20), kind=kOutput, calls=%fused_computation.19 | convolution fusion | flops 2147483648 | bytes 8388612 | tf_op jit(solution)/shard_map/mr,mn->rn/dot_general | solution.py:21
  64.0 0.0 collective-permute-done
  64.0 18.1 %collective-permute-done.2 = bf16[1024,512]{1,0:T(8,128)(2,1)} collective-permute-done((bf16[1024,512]{1,0:T(8,128)(2,1)}, bf16[1024,512]{1,0:T(8,128)(2,1)}, u32[]{:S(2)}, u32[]{:S(2)}) %collective-permute-start.2) | collective-permute-done | bytes 1048608 | tf_op jit(solution)/shard_map/ppermute | solution.py:54
  82.0 3.8 %all-gather.4.cloned.1.call-done = bf16[1024,1024]{1,0:T(8,128)(2,1)} async-done(((bf16[128,1024]{1,0:T(8,128)(2,1)}), bf16[1024,1024]{1,0:T(8,128)(2,1)}) %all-gather.4.cloned.1.call-update) | async-done | bytes 2097168 | tf_op jit(solution)/shard_map/all_gather | solution.py:28
  85.8 0.0 copy-done.1
  85.8 0.0 copy-start.5
  85.8 4.2 %fusion.1 = f32[1024,512]{1,0:T(8,128)S(1)} fusion(bf16[1024,1024]{1,0:T(8,128)(2,1)} %all-gather.4.cloned.1.call-done, f32[1024,512]{1,0:T(8,128)S(1)} %copy-done.1, bf16[1024,512]{1,0:T(8,128)(2,1)} %collective-permute-done.2, bf16[1024,512]{1,0:T(8,128)(2,1)S(1)} %collective-permute-done, f32[512,1024]{0,1:T(8,128)} %fusion.11), kind=kOutput, calls=%fused_computation.5 | convolution fusion | flops 1081606144 | bytes 10485760 | tf_op jit(solution)/shard_map/mr,mn->rn/dot_general | solution.py:21
  90.1 0.0 copy-start.4
  90.1 0.0 copy-start.2
  90.1 0.0 copy-start.3
  90.1 2.7 %broadcast_in_dim.3 = bf16[1024,2048]{1,0:T(8,128)(2,1)} broadcast(bf16[]{:T(256)} %constant.18.clone.1), dimensions={} | broadcast | bytes 4194306 | tf_op jit(solution)/shard_map/broadcast_in_dim | solution.py:67
  92.8 0.0 copy-done.5
  92.8 0.5 copy-done.2
  93.2 1.3 copy-done.3
  94.6 5.6 %constant_dynamic-update-slice_fusion.3 = (bf16[1024,2048]{1,0:T(8,128)(2,1)}, bf16[1024,512]{1,0:T(8,128)(2,1)}, f32[1024,512]{1,0:T(8,128)}) fusion(bf16[1024,2048]{1,0:T(8,128)(2,1)} %broadcast_in_dim.3, s32[]{:T(128)S(6)} %select_n.20, f32[1024,512]{1,0:T(8,128)S(1)} %fusion.1, bf16[1024,512]{1,0:T(8,128)(2,1)} %collective-permute-done.2, ...), kind=kOutput, calls=%fused_computation.32 | convolution fusion | flops 1079508992 | bytes 14680068 | tf_op jit(solution)/shard_map/mr,mn->rn/dot_general | solution.py:21
  100.1 0.0 copy-done.4
  100.1 1.2 collective-permute-start.4
  101.3 2.9 %collective-permute-start.3 = (bf16[1024,512]{1,0:T(8,128)(2,1)}, bf16[1024,512]{1,0:T(8,128)(2,1)S(1)}, u32[]{:S(2)}, u32[]{:S(2)}) collective-permute-start(bf16[1024,512]{1,0:T(8,128)(2,1)} %get-tuple-element.9), channel_id=1, source_target_pairs={{0,8},{8,0},{16,24},{24,16},{1,9},{9,1},{17,25},{25,17},{2,10},{10... | collective-permute-start | bytes 3145736 | tf_op jit(solution)/shard_map/ppermute | solution.py:65
  104.2 18.3 %collective-permute-done.4 = bf16[1024,512]{1,0:T(8,128)(2,1)S(1)} collective-permute-done((bf16[1024,512]{1,0:T(8,128)(2,1)}, bf16[1024,512]{1,0:T(8,128)(2,1)S(1)}, u32[]{:S(2)}, u32[]{:S(2)}) %collective-permute-start.4) | collective-permute-done | bytes 1048608 | tf_op jit(solution)/shard_map/ppermute | solution.py:64
  122.5 3.5 %collective-permute-start.5 = (bf16[1024,512]{1,0:T(8,128)(2,1)S(1)}, bf16[1024,512]{1,0:T(8,128)(2,1)S(1)}, u32[]{:S(2)}, u32[]{:S(2)}) collective-permute-start(bf16[1024,512]{1,0:T(8,128)(2,1)S(1)} %collective-permute-done.4), channel_id=1, source_target_pairs={{0,8},{8,0},{16,24},{24,16},{1,9},{9,1},{17,25},{25,17},{2,10},{10... | collective-permute-start | bytes 3145736 | tf_op jit(solution)/shard_map/ppermute | solution.py:66
  125.9 12.2 %copy.10 = bf16[2048,2048]{0,1:T(8,128)(2,1)} copy(bf16[2048,2048]{1,0:T(8,128)(2,1)} %param.6) | data formatting | bytes 16777216 | tf_op args[0]
  138.2 0.0 copy-start
  138.2 0.0 collective-permute-done.3
  138.2 1.0 constant_dynamic-update-slice_fusion.2
  139.2 1.0 constant_dynamic-update-slice_fusion.1
  140.2 0.0 collective-permute-done.5
  140.2 1.0 constant_dynamic-update-slice_fusion
  141.3 0.0 copy-done
  141.3 17.1 %fusion = (bf16[2048,2048]{0,1:T(8,128)(2,1)}, bf16[2048,2048]{1,0:T(8,128)(2,1)}) fusion(bf16[2048,2048]{0,1:T(8,128)(2,1)} %copy.10, bf16[1024,2048]{1,0:T(8,128)(2,1)} %constant_dynamic-update-slice_fusion, bf16[2048,1024]{1,0:T(8,128)(2,1)S(1)} %copy-done), kind=kOutput, calls=%fused_computation.1 | convolution fusion | flops 8610906112 | bytes 33554432 | tf_op jit(solution)/shard_map/dot_general | solution.py:77
  158.4 12.2 %copy.15 = bf16[2048,2048]{1,0:T(8,128)(2,1)} copy(bf16[2048,2048]{0,1:T(8,128)(2,1)} %get-tuple-element.11) | data formatting | bytes 16777216
  170.6 12.2 %copy.16 = bf16[2048,2048]{1,0:T(8,128)(2,1)} copy(bf16[2048,2048]{0,1:T(8,128)(2,1)} %bitcast.32) | data formatting | bytes 16777216
Async XLA Ops:
  7.2 29.2 %all-gather.6.cloned.1.call-start = ((), (), s32[]{:S(2)}) async-start(), calls=%async_computation.1 | async-start | bytes 2621440 | tf_op jit(solution)/shard_map/all_gather | solution.py:27
  11.2 74.7 %all-gather.4.cloned.1.call-start = ((), (), s32[]{:S(2)}) async-start(), calls=%async_computation | async-start | bytes 2359296 | tf_op jit(solution)/shard_map/all_gather | solution.py:28
  44.1 6.9 %collective-permute-start.1 = (bf16[1024,512]{1,0:T(8,128)(2,1)S(1)}, bf16[1024,512]{1,0:T(8,128)(2,1)S(1)}, u32[]{:S(2)}, u32[]{:S(2)}) collective-permute-start(bf16[1024,512]{1,0:T(8,128)(2,1)S(1)} %fusion.21), channel_id=1, source_target_pairs={{0,8},{8,0},{16,24},{24,16},{1,9},{9,1},{17,25},{25,17},{2,10},{10... | collective-permute-start | bytes 3145736 | tf_op jit(solution)/shard_map/ppermute | solution.py:52
  50.8 13.2 %collective-permute-start = (bf16[1024,512]{1,0:T(8,128)(2,1)}, bf16[1024,512]{1,0:T(8,128)(2,1)S(1)}, u32[]{:S(2)}, u32[]{:S(2)}) collective-permute-start(bf16[1024,512]{1,0:T(8,128)(2,1)} %fusion.24), channel_id=1, source_target_pairs={{0,8},{8,0},{16,24},{24,16},{1,9},{9,1},{17,25},{25,17},{2,10},{10... | collective-permute-start | bytes 3145736 | tf_op jit(solution)/shard_map/ppermute | solution.py:55
  57.3 24.8 %collective-permute-start.2 = (bf16[1024,512]{1,0:T(8,128)(2,1)}, bf16[1024,512]{1,0:T(8,128)(2,1)}, u32[]{:S(2)}, u32[]{:S(2)}) collective-permute-start(bf16[1024,512]{1,0:T(8,128)(2,1)} %fusion.3), channel_id=1, source_target_pairs={{0,16},{8,24},{16,0},{24,8},{1,17},{9,25},{17,1},{25,9},{2,18},{10... | collective-permute-start | bytes 3145736 | tf_op jit(solution)/shard_map/ppermute | solution.py:54
  57.3 28.6 %copy-start.1 = (f32[1024,512]{1,0:T(8,128)S(1)}, f32[1024,512]{1,0:T(8,128)}, u32[]{:S(2)}) copy-start(f32[1024,512]{1,0:T(8,128)} %param.11) | copy-start | bytes 6291460
  85.8 6.9 %copy-start.5 = (f32[512,1024]{0,1:T(8,128)S(1)}, f32[512,1024]{0,1:T(8,128)}, u32[]{:S(2)}) copy-start(f32[512,1024]{0,1:T(8,128)} %fusion.11) | copy-start | bytes 6291460
  90.1 10.1 %copy-start.4 = (f32[1024,512]{1,0:T(8,128)}, f32[1024,512]{1,0:T(8,128)S(1)}, u32[]{:S(2)}) copy-start(f32[1024,512]{1,0:T(8,128)S(1)} %fusion.1) | copy-start | bytes 6291460
  90.1 3.2 %copy-start.2 = (f32[1024,512]{1,0:T(8,128)S(1)}, f32[1024,512]{1,0:T(8,128)}, u32[]{:S(2)}) copy-start(f32[1024,512]{1,0:T(8,128)} %param.10) | copy-start | bytes 6291460
  90.1 4.5 %copy-start.3 = (bf16[1024,1024]{1,0:T(8,128)(2,1)S(1)}, bf16[1024,1024]{1,0:T(8,128)(2,1)}, u32[]{:S(2)}) copy-start(bf16[1024,1024]{1,0:T(8,128)(2,1)} %all-gather.4.cloned.1.call-done) | copy-start | bytes 6291460
  100.1 22.3 %collective-permute-start.4 = (bf16[1024,512]{1,0:T(8,128)(2,1)}, bf16[1024,512]{1,0:T(8,128)(2,1)S(1)}, u32[]{:S(2)}, u32[]{:S(2)}) collective-permute-start(bf16[1024,512]{1,0:T(8,128)(2,1)} %get-tuple-element.9), channel_id=1, source_target_pairs={{0,16},{8,24},{16,0},{24,8},{1,17},{9,25},{17,1},{25,9},{2,18},{10... | collective-permute-start | bytes 3145736 | tf_op jit(solution)/shard_map/ppermute | solution.py:64
  101.3 36.8 %collective-permute-start.3 = (bf16[1024,512]{1,0:T(8,128)(2,1)}, bf16[1024,512]{1,0:T(8,128)(2,1)S(1)}, u32[]{:S(2)}, u32[]{:S(2)}) collective-permute-start(bf16[1024,512]{1,0:T(8,128)(2,1)} %get-tuple-element.9), channel_id=1, source_target_pairs={{0,8},{8,0},{16,24},{24,16},{1,9},{9,1},{17,25},{25,17},{2,10},{10... | collective-permute-start | bytes 3145736 | tf_op jit(solution)/shard_map/ppermute | solution.py:65
  122.5 17.8 %collective-permute-start.5 = (bf16[1024,512]{1,0:T(8,128)(2,1)S(1)}, bf16[1024,512]{1,0:T(8,128)(2,1)S(1)}, u32[]{:S(2)}, u32[]{:S(2)}) collective-permute-start(bf16[1024,512]{1,0:T(8,128)(2,1)S(1)} %collective-permute-done.4), channel_id=1, source_target_pairs={{0,8},{8,0},{16,24},{24,16},{1,9},{9,1},{17,25},{25,17},{2,10},{10... | collective-permute-start | bytes 3145736 | tf_op jit(solution)/shard_map/ppermute | solution.py:66
  138.2 3.1 %copy-start = (bf16[2048,1024]{1,0:T(8,128)(2,1)S(1)}, bf16[2048,1024]{1,0:T(8,128)(2,1)}, u32[]{:S(2)}) copy-start(bf16[2048,1024]{1,0:T(8,128)(2,1)} %param.9) | copy-start | bytes 12582916
Sparse Core Ops, SparseCore 0:
  11.3 25.0 all-gather.5
  39.0 46.7 all-gather.3
